TPU v7x, 128 devices: a whole 4x4x4 slice. The times are simulated.
128 devices in a mesh: section: 8 (over x, core), expert: 16 (over z, y).
Axes of the slice: x: 4, y: 4, z: 4, core: 2. Of those that a mesh axis runs over, the one named last changes fastest.
Arguments:
- sent_acts: bfloat16 [8, 2048, 6144], P('section', 'expert'), may hold values from -6 to 6
- sent_cots: bfloat16 [8, 2048, 6144], P('section', 'expert'), may hold values from -6 to 6
- expert_ids: int32 [8, 2048, 2], P('section', 'expert'), may hold values from 0 to 7, as said below
- gate_probs: float32 [8, 2048, 2], P('section', 'expert'), may hold values from 0.1 to 0.9
- gate_weight: bfloat16 [8, 6144, 8192], P('section', None, 'expert'), may hold values from -0.078125 to 0.078125
- up_weight: bfloat16 [8, 6144, 8192], P('section', None, 'expert'), may hold values from -0.078125 to 0.078125
- down_weight: bfloat16 [8, 8192, 6144], P('section', 'expert'), may hold values from -0.0625 to 0.0625
Outputs:
- out_acts: bfloat16 [8, 2048, 6144], P('section', 'expert')
- in_grads: bfloat16 [8, 2048, 6144], P('section', 'expert')
Inputs may be any that keep to these rules, and one draw needn't show every extreme that they name: `expert_ids`: in every section, at most 40 of the 128 tokens of one device name expert 0, and at least one device's tokens name it 40 times; a token's two experts differ.
All inputs are finite; a program needn't handle non-finite values.
Results may differ from a plain program's by a relative error of at most 0.015.
Values may be sent and summed in bfloat16 or wider, within the bound.
A program may use at most 128 MiB of HBM per device.

v0:
```python
import jax
import jax.numpy as jnp
from jax import lax
from jax.sharding import PartitionSpec as P

CAP = 40


def shifted(value, axis, steps):
    count = lax.axis_size(axis)
    pairs = [(source, (source + steps) % count) for source in range(count)]
    return lax.ppermute(value, axis, pairs)


def silu_grad(pre):
    sigma = jax.nn.sigmoid(pre)
    return sigma * (1.0 + pre * (1.0 - sigma))


def run_rows(kernel, inputs):
    return kernel(*inputs)


def combine(term_rows):
    return lax.psum_scatter(
        term_rows(jnp.int32(0), lax.axis_size("expert") * CAP).astype(jnp.bfloat16),
        "expert",
        scatter_dimension=0,
        tiled=True,
    ).astype(jnp.float32)


def body(sent_acts, sent_cots, expert_ids, gate_probs, gate_weight, up_weight, down_weight):
    tok_count = sent_acts.shape[1]
    gate_cols = gate_weight[0]
    up_cols = up_weight[0]
    down_rows = down_weight[0]
    contract = (((1,), (1,)), ((), ()))
    incoming = shifted(sent_acts[0], "section", 1)
    cot_in = shifted(sent_cots[0], "section", -1)
    chosen = expert_ids[0] == 0
    picked = jnp.any(chosen, axis=1)
    picked_int = picked.astype(jnp.int32)
    share = jnp.sum(jnp.where(chosen, gate_probs[0], 0.0), axis=1)
    ranking = jnp.cumsum(picked_int) - picked_int
    slot_of = jnp.where(picked, ranking, CAP)
    table = (
        jnp.full((CAP + 1,), -1, jnp.int32)
        .at[slot_of]
        .set(jnp.arange(tok_count, dtype=jnp.int32))[:CAP]
    )
    filled_slot = table >= 0
    source = jnp.maximum(table, 0)
    slot_acts = jnp.where(filled_slot[:, None], incoming[source], jnp.zeros((), incoming.dtype))
    all_acts = lax.all_gather(slot_acts, "expert", axis=0, tiled=True)

    def forward_rows(rows_in):
        pre_gate = jnp.dot(rows_in, gate_cols, preferred_element_type=jnp.float32)
        pre_up = jnp.dot(rows_in, up_cols, preferred_element_type=jnp.float32)
        hidden = (jax.nn.silu(pre_gate) * pre_up).astype(jnp.bfloat16)
        return (pre_gate, pre_up, hidden)

    pre_gate, pre_up, hidden = run_rows(forward_rows, (all_acts,))

    def forward_term(start, count):
        return jnp.dot(hidden, down_rows, preferred_element_type=jnp.float32)

    slot_out = combine(forward_term)
    back_index = jnp.minimum(slot_of, CAP - 1)
    out_acts = jnp.where(picked[:, None], share[:, None] * slot_out[back_index], 0.0).astype(
        jnp.bfloat16
    )
    out_grad = (cot_in.astype(jnp.float32) * share[:, None]).astype(jnp.bfloat16)
    slot_grads = jnp.where(filled_slot[:, None], out_grad[source], jnp.zeros((), out_grad.dtype))
    all_grads = lax.all_gather(slot_grads, "expert", axis=0, tiled=True)

    def backward_rows(gate_in, up_in, grads_in):
        hid_grad = lax.dot_general(
            grads_in, down_rows, contract, preferred_element_type=jnp.float32
        )
        gate_grad = (hid_grad * up_in * silu_grad(gate_in)).astype(jnp.bfloat16)
        up_grad = (hid_grad * jax.nn.silu(gate_in)).astype(jnp.bfloat16)
        return (gate_grad, up_grad)

    gate_grad, up_grad = run_rows(backward_rows, (pre_gate, pre_up, all_grads))

    def backward_term(start, count):
        term = lax.dot_general(gate_grad, gate_cols, contract, preferred_element_type=jnp.float32)
        return term + lax.dot_general(
            up_grad, up_cols, contract, preferred_element_type=jnp.float32
        )

    slot_back = combine(backward_term)
    in_grads = jnp.where(picked[:, None], slot_back[back_index], 0.0).astype(jnp.bfloat16)
    return (out_acts[None], in_grads[None])


def solution(mesh):
    placed = (
        P("section", "expert", None),
        P("section", "expert", None),
        P("section", "expert", None),
        P("section", "expert", None),
        P("section", None, "expert"),
        P("section", None, "expert"),
        P("section", "expert", None),
    )
    return jax.shard_map(
        body,
        mesh=mesh,
        in_specs=placed,
        out_specs=(P("section", "expert", None), P("section", "expert", None)),
        check_vma=False,
    )
```

profile of v0, /device:TPU:0, one launch (start us, length us, event | category | flops | bytes accessed | tf_op | source)
XLA Modules:
  0.0 397.2 jit_solution(13419910968165939987)
XLA Ops:
  7.2 0.0 all-gather.3.cloned.1.call-start
  7.2 2.3 collective-permute-start.1
  9.5 0.0 collective-permute-start
  9.5 0.7 fusion.21
  10.2 0.1 copy.14
  10.4 0.2 reduce-window.4
  10.6 0.1 fusion.18
  10.7 1.0 scatter_custom_fusion
  11.7 0.7 select_reduce_fusion
  12.4 15.4 %collective-permute-done.1 = bf16[128,6144]{1,0:T(8,128)(2,1)} collective-permute-done((bf16[128,6144]{1,0:T(8,128)(2,1)}, bf16[128,6144]{1,0:T(8,128)(2,1)}, u32[]{:S(2)}, u32[]{:S(2)}) %collective-permute-start.1) | collective-permute-done | bytes 1572896 | tf_op jit(solution)/shard_map/ppermute | solution.py:12
  27.8 1.8 multiply_convert_fusion
  29.5 1.6 gather_fusion.2
  31.2 0.0 copy-start
  31.2 0.0 collective-permute-done
  31.2 0.8 gather_fusion
  32.0 0.2 copy-done
  32.2 1.1 broadcast_select_fusion
  33.3 0.0 all-gather.3.cloned.1.call-update
  33.3 0.0 all-gather.5.cloned.1.call-start
  33.3 0.7 all-gather.5.cloned.1.call-update
  34.1 0.0 reduce-scatter.9.cloned.1.call-start
  34.1 70.5 %all-gather.3.cloned.1.call-done = bf16[640,6144]{1,0:T(8,128)(2,1)} async-done(((bf16[40,6144]{1,0:T(8,128)(2,1)}), bf16[640,6144]{1,0:T(8,128)(2,1)}) %all-gather.3.cloned.1.call-update) | async-done | bytes 7864336 | tf_op jit(solution)/shard_map/all_gather | solution.py:55
  104.6 0.0 copy-start.2
  104.6 8.5 %fusion.8 = f32[640,512]{1,0:T(8,128)S(1)} fusion(bf16[640,6144]{1,0:T(8,128)(2,1)} %all-gather.3.cloned.1.call-done, bf16[1,6144,512]{2,1,0:T(8,128)(2,1)} %param.11), kind=kOutput, calls=%fused_computation.15 | convolution fusion | flops 4026531840 | bytes 15466496 | tf_op jit(solution)/shard_map/dot_general | solution.py:58
  113.1 0.0 copy-done.2
  113.1 6.4 %fusion.4 = f32[640,512]{1,0:T(8,128)S(1)} fusion(bf16[640,6144]{1,0:T(8,128)(2,1)S(1)} %copy-done.2, bf16[1,6144,512]{2,1,0:T(8,128)(2,1)} %param.12), kind=kOutput, calls=%fused_computation.11 | convolution fusion | flops 4026531840 | bytes 15466496 | tf_op jit(solution)/shard_map/dot_general | solution.py:59
  119.6 56.0 %all-gather.5.cloned.1.call-done = bf16[640,6144]{1,0:T(8,128)(2,1)} async-done(((bf16[40,6144]{1,0:T(8,128)(2,1)}), bf16[640,6144]{1,0:T(8,128)(2,1)}) %all-gather.5.cloned.1.call-update) | async-done | bytes 7864336 | tf_op jit(solution)/shard_map/all_gather | solution.py:75
  175.6 8.5 %fusion = f32[640,512]{1,0:T(8,128)S(1)} fusion(bf16[640,6144]{1,0:T(8,128)(2,1)} %all-gather.5.cloned.1.call-done, bf16[1,512,6144]{2,1,0:T(8,128)(2,1)} %param.13), kind=kOutput, calls=%fused_computation.7 | convolution fusion | flops 4026531840 | bytes 15466496 | tf_op jit(solution)/shard_map/dot_general | solution.py:78
  184.0 0.0 copy-start.1
  184.0 1.0 copy-done.1
  185.1 10.6 %fusion.6 = f32[640,6144]{1,0:T(8,128)} fusion(bf16[1,6144,512]{2,1,0:T(8,128)(2,1)} %param.11, f32[640,512]{1,0:T(8,128)S(1)} %fusion.8, f32[640,512]{1,0:T(8,128)S(1)} %fusion, f32[640,512]{1,0:T(8,128)S(1)} %fusion.4), kind=kOutput, calls=%fused_computation.13 | convolution fusion | flops 4029808640 | bytes 25952256 | tf_op jit(solution)/shard_map/dot_general | solution.py:88
  195.7 15.1 %add_convert_fusion = bf16[640,6144]{1,0:T(8,128)(2,1)} fusion(f32[640,6144]{1,0:T(8,128)} %fusion.6, bf16[1,6144,512]{2,1,0:T(8,128)(2,1)} %param.12, f32[640,512]{1,0:T(8,128)} %copy-done.1, f32[640,512]{1,0:T(8,128)S(1)} %fusion.8), kind=kOutput, calls=%fused_computation.5 | convolution fusion | flops 4036362240 | bytes 32505856 | tf_op jit(solution)/shard_map/dot_general | solution.py:89
  210.7 0.0 reduce-scatter.9.cloned.1.call-update
  210.8 0.2 reduce-scatter.7.cloned.1.call-start
  211.0 9.2 %convolution_convert_fusion = bf16[640,6144]{1,0:T(8,128)(2,1)} fusion(bf16[1,512,6144]{2,1,0:T(8,128)(2,1)} %param.13, f32[640,512]{1,0:T(8,128)S(1)} %fusion.4, f32[640,512]{1,0:T(8,128)S(1)} %fusion.8), kind=kOutput, calls=%fused_computation.6 | convolution fusion | flops 4032430080 | bytes 16777216 | tf_op jit(solution)/shard_map/dot_general | solution.py:66
  220.2 0.0 reduce-scatter.7.cloned.1.call-update
  220.2 75.2 %reduce-scatter.9.cloned.1.call-done = bf16[40,6144]{1,0:T(8,128)(2,1)} async-done(((bf16[640,6144]{1,0:T(8,128)(2,1)}), bf16[40,6144]{1,0:T(8,128)(2,1)}) %reduce-scatter.9.cloned.1.call-update) | async-done | bytes 491536
  295.4 4.1 %gather_fusion.3 = bf16[128,6144]{1,0:T(8,128)(2,1)S(1)} fusion(bf16[40,6144]{1,0:T(8,128)(2,1)} %reduce-scatter.9.cloned.1.call-done, s32[1024]{0:T(1024)S(1)} %pad_clamp_fusion), kind=kCustom, calls=%fused_computation.3 | custom fusion | bytes 3146240 | tf_op jit(solution)/shard_map/gather | solution.py:94
  299.5 1.5 fusion.10
  301.0 81.9 %reduce-scatter.7.cloned.1.call-done = bf16[40,6144]{1,0:T(8,128)(2,1)} async-done(((bf16[640,6144]{1,0:T(8,128)(2,1)}), bf16[40,6144]{1,0:T(8,128)(2,1)}) %reduce-scatter.7.cloned.1.call-update) | async-done | bytes 491536
  383.0 1.1 convert_element_type.68
  384.1 3.2 gather_fusion.1
  387.2 3.4 fusion.12
  (6 shorter events, 0.0 us)
Async XLA Ops:
  7.2 97.4 %all-gather.3.cloned.1.call-start = ((), (), s32[]{:S(2)}) async-start(), calls=%async_computation.2 | async-start | bytes 8355840 | tf_op jit(solution)/shard_map/all_gather | solution.py:55
  7.2 20.6 %collective-permute-start.1 = (bf16[128,6144]{1,0:T(8,128)(2,1)}, bf16[128,6144]{1,0:T(8,128)(2,1)}, u32[]{:S(2)}, u32[]{:S(2)}) collective-permute-start(bf16[128,6144]{1,0:T(8,128)(2,1)} %bitcast.33), channel_id=1, source_target_pairs={{0,112},{16,0},{32,16},{48,32},{64,48},{80,64},{96,80},{112,96},{1... | collective-permute-start | bytes 4718600 | tf_op jit(solution)/shard_map/ppermute | solution.py:12
  9.5 21.6 %collective-permute-start = (bf16[128,6144]{1,0:T(8,128)(2,1)}, bf16[128,6144]{1,0:T(8,128)(2,1)S(1)}, u32[]{:S(2)}, u32[]{:S(2)}) collective-permute-start(bf16[128,6144]{1,0:T(8,128)(2,1)} %bitcast.34), channel_id=1, source_target_pairs={{0,16},{16,32},{32,48},{48,64},{64,80},{80,96},{96,112},{112,0},{1... | collective-permute-start | bytes 4718600 | tf_op jit(solution)/shard_map/ppermute | solution.py:12
  31.2 1.0 copy-start
  33.3 142.3 %all-gather.5.cloned.1.call-start = ((), (), s32[]{:S(2)}) async-start(), calls=%async_computation.3 | async-start | bytes 8355840 | tf_op jit(solution)/shard_map/all_gather | solution.py:75
  34.1 261.4 %reduce-scatter.9.cloned.1.call-start = ((), (), s32[]{:S(2)}) async-start(), calls=%async_computation.5 | async-start | bytes 8355840
  104.6 8.5 %copy-start.2 = (bf16[640,6144]{1,0:T(8,128)(2,1)S(1)}, bf16[640,6144]{1,0:T(8,128)(2,1)}, u32[]{:S(2)}) copy-start(bf16[640,6144]{1,0:T(8,128)(2,1)} %all-gather.3.cloned.1.call-done) | copy-start | bytes 23592964
  184.0 1.1 copy-start.1
  210.8 172.2 %reduce-scatter.7.cloned.1.call-start = ((), (), s32[]{:S(2)}) async-start(), calls=%async_computation.4 | async-start | bytes 8355840
Sparse Core Ops, SparseCore 0:
  33.4 71.1 all-gather.2
  107.3 68.1 all-gather.4
  210.9 84.4 reduce-scatter.8
  298.8 84.1 reduce-scatter.6
where the time goes:
time: 398 us; the launch traced here: 397 us
  waiting for transfers between devices  300 us (75%)
  matrix products  58.3 us (15%)
  between operations  13.9 us (3%)
  local copies, waits for them, and re-layouts  12.1 us (3%)
  other arithmetic  10.6 us (3%)
    unnamed x6, waiting for transfers between devices  158 us
    all_gather x1, waiting for transfers between devices, body(): all_acts = lax.all_gather(slot_acts, 'expert', axis=0, tiled=True)  70.5 us
    all_gather x1, waiting for transfers between devices, body(): all_grads = lax.all_gather(slot_grads, 'expert', axis=0, tiled=True)  56 us
    ppermute x2, waiting for transfers between devices, shifted(): return lax.ppermute(value, axis, pairs)  15.4 us
    dot_general x1, matrix products, backward_term(): lax.dot_general(up_grad, up_cols, contract, preferred_element_type=jnp.fl...  15.1 us
    dot_general x1, matrix products, backward_term(): lax.dot_general(gate_grad, gate_cols, contract, preferred_element_type=jn...  10.6 us
    dot_general x1, matrix products, forward_term(): return jnp.dot(hidden, down_rows, preferred_element_type=jnp.float32)  9.21 us
    dot_general x1, matrix products, forward_rows(): pre_gate = jnp.dot(rows_in, gate_cols, preferred_element_type=jnp.float32)  8.51 us
  transfers between devices with their start and end apart: 6, of which 5 were waited for; matrix products, arithmetic and copies ran while one was open for 9% of the time, Pallas kernels for 0%

commit v1 on v0

--- a/solution.py
+++ b/solution.py
@@ -4,6 +4,12 @@
 from jax.sharding import PartitionSpec as P
 
 CAP = 40
+
+
+def gather_from_all(x, axis, dim):
+    length = lax.axis_size(axis)
+    repeats = [length if d == dim else 1 for d in range(x.ndim)]
+    return lax.all_to_all(jnp.tile(x, repeats), axis, split_axis=dim, concat_axis=dim, tiled=True)
 
 
 def shifted(value, axis, steps):
@@ -52,7 +58,7 @@
     filled_slot = table >= 0
     source = jnp.maximum(table, 0)
     slot_acts = jnp.where(filled_slot[:, None], incoming[source], jnp.zeros((), incoming.dtype))
-    all_acts = lax.all_gather(slot_acts, "expert", axis=0, tiled=True)
+    all_acts = gather_from_all(slot_acts, "expert", 0)
 
     def forward_rows(rows_in):
         pre_gate = jnp.dot(rows_in, gate_cols, preferred_element_type=jnp.float32)

time: 398 us -> 358 us (0.90)
  waiting for transfers between devices: 300 us -> 156 us
  blocking collectives: 0 us -> 111 us
  matrix products: 58.3 us -> 50.3 us
    all_to_all x0 -> x1, blocking collectives: none -> 111 us  [gather_from_all(): lax.all_to_all(jnp.tile(x, repeats), axis, split_axis=dim, concat_axis=di...]
    all_gather x1 -> x0, waiting for transfers between devices: 70.5 us -> none  [body(): all_acts = lax.all_gather(slot_acts, 'expert', axis=0, tiled=True)]
    all_gather x1, waiting for transfers between devices: 56 us -> 9.35 us  [body(): all_grads = lax.all_gather(slot_grads, 'expert', axis=0, tiled=True)]
    unnamed x6 -> x5, waiting for transfers between devices: 158 us -> 131 us
    dot_general x1, matrix products: 8.51 us -> 4.26 us  [forward_rows(): pre_gate = jnp.dot(rows_in, gate_cols, preferred_element_type=jnp.float32)]
  transfers between devices with their start and end apart: 6 -> 5, of which waited for: 5 -> 4; matrix products, arithmetic and copies ran while one was open for 9% -> 18% of each run, Pallas kernels for 0% -> 0%
where the time goes in v1:
time: 358 us
  waiting for transfers between devices  156 us (44%)
  blocking collectives  111 us (31%)
  matrix products  50.3 us (14%)
  between operations  13.9 us (4%)
  local copies, waits for them, and re-layouts  13.1 us (4%)
  other arithmetic  10.4 us (3%)
    unnamed x5, waiting for transfers between devices  131 us
    all_to_all x1, blocking collectives, gather_from_all(): lax.all_to_all(jnp.tile(x, repeats), axis, split_axis=dim, concat_axis=di...  111 us
    dot_general x1, matrix products, backward_term(): lax.dot_general(up_grad, up_cols, contract, preferred_element_type=jnp.fl...  15.8 us
    ppermute x2, waiting for transfers between devices, shifted(): return lax.ppermute(value, axis, pairs)  15.4 us
    dot_general x1, matrix products, backward_term(): lax.dot_general(gate_grad, gate_cols, contract, preferred_element_type=jn...  11 us
    all_gather x1, waiting for transfers between devices, body(): all_grads = lax.all_gather(slot_grads, 'expert', axis=0, tiled=True)  9.35 us
    dot_general x1, matrix products, backward_rows(): lax.dot_general(grads_in, down_rows, contract, preferred_element_type=jnp...  8.45 us
  transfers between devices with their start and end apart: 5, of which 4 were waited for; matrix products, arithmetic and copies ran while one was open for 18% of the time, Pallas kernels for 0%

profile of v1, /device:TPU:0, one launch (start us, length us, event | category | flops | bytes accessed | tf_op | source)
XLA Modules:
  0.0 357.6 jit_solution(16803776809343478851)
XLA Ops:
  7.2 0.0 all-gather.2.cloned.1.call-start
  7.2 2.3 collective-permute-start.1
  9.5 0.0 collective-permute-start
  9.5 0.7 fusion.21
  10.2 0.1 copy.14
  10.4 0.2 reduce-window.4
  10.6 0.1 fusion.18
  10.7 1.0 scatter_custom_fusion
  11.7 0.7 select_reduce_fusion
  12.4 15.4 %collective-permute-done.1 = bf16[128,6144]{1,0:T(8,128)(2,1)} collective-permute-done((bf16[128,6144]{1,0:T(8,128)(2,1)}, bf16[128,6144]{1,0:T(8,128)(2,1)}, u32[]{:S(2)}, u32[]{:S(2)}) %collective-permute-start.1) | collective-permute-done | bytes 1572896 | tf_op jit(solution)/shard_map/ppermute | solution.py:18
  27.8 1.8 multiply_convert_fusion
  29.5 1.6 gather_fusion.2
  31.2 0.0 copy-start
  31.2 0.0 collective-permute-done
  31.2 0.8 gather_fusion
  32.0 0.2 copy-done
  32.2 0.9 broadcast_select_fusion
  33.1 0.0 all-gather.2.cloned.1.call-update
  33.1 0.0 reduce-scatter.7.cloned.1.call-start
  33.2 0.0 slice-start
  33.2 1.0 tile.2
  34.2 0.0 slice-start.1
  34.2 0.0 slice-start.4
  34.2 111.5 %all_to_all.9 = bf16[16,40,6144]{2,1,0:T(8,128)(2,1)S(1)} all-to-all(bf16[16,40,6144]{2,1,0:T(8,128)(2,1)S(1)} %tile.2), channel_id=1, replica_groups=mesh['section'=8,'expert'=16] {'expert'}, dimensions={0} | all-to-all | bytes 15728640 | tf_op jit(solution)/shard_map/all_to_all | solution.py:12
  145.7 0.0 slice-done
  145.7 0.0 slice-done.1
  145.7 0.0 slice-start.5
  145.7 0.0 slice-start.2
  145.7 4.3 %fusion.8 = f32[640,512]{1,0:T(8,128)S(1)} fusion(bf16[640,6144]{1,0:T(8,128)(2,1)S(1)} %bitcast.33, bf16[1,6144,512]{2,1,0:T(8,128)(2,1)S(1)} %bitcast.36), kind=kOutput, calls=%fused_computation.15 | convolution fusion | flops 4026531840 | bytes 15466496 | tf_op jit(solution)/shard_map/dot_general | solution.py:64
  150.0 0.0 slice-done.4
  150.0 0.0 slice-done.5
  150.0 0.0 slice-start.3
  150.0 4.2 %fusion.4 = f32[640,512]{1,0:T(8,128)S(1)} fusion(bf16[640,6144]{1,0:T(8,128)(2,1)S(1)} %bitcast.34, bf16[1,6144,512]{2,1,0:T(8,128)(2,1)S(1)} %bitcast.41), kind=kOutput, calls=%fused_computation.11 | convolution fusion | flops 4026531840 | bytes 15466496 | tf_op jit(solution)/shard_map/dot_general | solution.py:65
  154.2 0.0 slice-done.2
  154.2 0.0 slice-done.3
  154.2 6.5 %convolution_convert_fusion = bf16[640,6144]{1,0:T(8,128)(2,1)} fusion(bf16[1,512,6144]{2,1,0:T(8,128)(2,1)S(1)} %bitcast.39, f32[640,512]{1,0:T(8,128)S(1)} %fusion.4, f32[640,512]{1,0:T(8,128)S(1)} %fusion.8), kind=kOutput, calls=%fused_computation.6 | convolution fusion | flops 4032430080 | bytes 16777216 | tf_op jit(solution)/shard_map/dot_general | solution.py:72
  160.7 0.0 reduce-scatter.7.cloned.1.call-update
  160.8 0.2 reduce-scatter.9.cloned.1.call-start
  161.0 9.3 %all-gather.2.cloned.1.call-done = bf16[640,6144]{1,0:T(8,128)(2,1)} async-done(((bf16[40,6144]{1,0:T(8,128)(2,1)}), bf16[640,6144]{1,0:T(8,128)(2,1)}) %all-gather.2.cloned.1.call-update) | async-done | bytes 7864336 | tf_op jit(solution)/shard_map/all_gather | solution.py:81
  170.3 8.5 %fusion = f32[640,512]{1,0:T(8,128)S(1)} fusion(bf16[640,6144]{1,0:T(8,128)(2,1)} %all-gather.2.cloned.1.call-done, bf16[1,512,6144]{2,1,0:T(8,128)(2,1)} %param.13), kind=kOutput, calls=%fused_computation.7 | convolution fusion | flops 4026531840 | bytes 15466496 | tf_op jit(solution)/shard_map/dot_general | solution.py:84
  178.8 0.0 copy-start.1
  178.8 1.0 copy-done.1
  179.9 11.0 %fusion.6 = f32[640,6144]{1,0:T(8,128)} fusion(bf16[1,6144,512]{2,1,0:T(8,128)(2,1)} %param.11, f32[640,512]{1,0:T(8,128)S(1)} %fusion.8, f32[640,512]{1,0:T(8,128)S(1)} %fusion, f32[640,512]{1,0:T(8,128)S(1)} %fusion.4), kind=kOutput, calls=%fused_computation.13 | convolution fusion | flops 4029808640 | bytes 25952256 | tf_op jit(solution)/shard_map/dot_general | solution.py:94
  190.9 15.8 %add_convert_fusion = bf16[640,6144]{1,0:T(8,128)(2,1)} fusion(f32[640,6144]{1,0:T(8,128)} %fusion.6, bf16[1,6144,512]{2,1,0:T(8,128)(2,1)} %param.12, f32[640,512]{1,0:T(8,128)} %copy-done.1, f32[640,512]{1,0:T(8,128)S(1)} %fusion.8), kind=kOutput, calls=%fused_computation.5 | convolution fusion | flops 4036362240 | bytes 32505856 | tf_op jit(solution)/shard_map/dot_general | solution.py:95
  206.7 0.0 reduce-scatter.9.cloned.1.call-update
  206.8 51.0 %reduce-scatter.7.cloned.1.call-done = bf16[40,6144]{1,0:T(8,128)(2,1)} async-done(((bf16[640,6144]{1,0:T(8,128)(2,1)}), bf16[40,6144]{1,0:T(8,128)(2,1)}) %reduce-scatter.7.cloned.1.call-update) | async-done | bytes 491536
  257.7 1.1 convert_element_type.68
  258.8 3.2 gather_fusion.1
  262.0 3.4 fusion.12
  265.4 80.1 %reduce-scatter.9.cloned.1.call-done = bf16[40,6144]{1,0:T(8,128)(2,1)} async-done(((bf16[640,6144]{1,0:T(8,128)(2,1)}), bf16[40,6144]{1,0:T(8,128)(2,1)}) %reduce-scatter.9.cloned.1.call-update) | async-done | bytes 491536
  345.5 4.1 %gather_fusion.3 = bf16[128,6144]{1,0:T(8,128)(2,1)S(1)} fusion(bf16[40,6144]{1,0:T(8,128)(2,1)} %reduce-scatter.9.cloned.1.call-done, s32[1024]{0:T(1024)S(1)} %pad_clamp_fusion), kind=kCustom, calls=%fused_computation.3 | custom fusion | bytes 3146240 | tf_op jit(solution)/shard_map/gather | solution.py:100
  349.6 1.5 fusion.10
  (9 shorter events, 0.0 us)
Async XLA Ops:
  7.2 163.2 %all-gather.2.cloned.1.call-start = ((), (), s32[]{:S(2)}) async-start(), calls=%async_computation.3 | async-start | bytes 8355840 | tf_op jit(solution)/shard_map/all_gather | solution.py:81
  7.2 20.6 %collective-permute-start.1 = (bf16[128,6144]{1,0:T(8,128)(2,1)}, bf16[128,6144]{1,0:T(8,128)(2,1)}, u32[]{:S(2)}, u32[]{:S(2)}) collective-permute-start(bf16[128,6144]{1,0:T(8,128)(2,1)} %bitcast.42), channel_id=1, source_target_pairs={{0,112},{16,0},{32,16},{48,32},{64,48},{80,64},{96,80},{112,96},{1... | collective-permute-start | bytes 4718600 | tf_op jit(solution)/shard_map/ppermute | solution.py:18
  9.5 21.6 %collective-permute-start = (bf16[128,6144]{1,0:T(8,128)(2,1)}, bf16[128,6144]{1,0:T(8,128)(2,1)S(1)}, u32[]{:S(2)}, u32[]{:S(2)}) collective-permute-start(bf16[128,6144]{1,0:T(8,128)(2,1)} %bitcast.43), channel_id=1, source_target_pairs={{0,16},{16,32},{32,48},{48,64},{64,80},{80,96},{96,112},{112,0},{1... | collective-permute-start | bytes 4718600 | tf_op jit(solution)/shard_map/ppermute | solution.py:18
  31.2 1.0 copy-start
  33.1 224.6 %reduce-scatter.7.cloned.1.call-start = ((), (), s32[]{:S(2)}) async-start(), calls=%async_computation.4 | async-start | bytes 8355840
  33.2 112.5 %slice-start = ((s8[6291456]{0:T(1024)(128)(4,1)}), s8[4194304]{0:T(1024)(128)(4,1)S(1)}, s32[]{:S(2)}) async-start(s8[6291456]{0:T(1024)(128)(4,1)} %bitcast.35), calls=%async_computation.6 | async-start | bytes 8388608
  34.2 111.5 %slice-start.1 = ((s8[6291456]{0:T(1024)(128)(4,1)}), s8[2097152]{0:T(1024)(128)(4,1)S(1)}, s32[]{:S(2)}) async-start(s8[6291456]{0:T(1024)(128)(4,1)} %bitcast.35), calls=%async_computation.7 | async-start | bytes 4194304
  34.2 115.8 %slice-start.4 = ((s8[6291456]{0:T(1024)(128)(4,1)}), s8[4194304]{0:T(1024)(128)(4,1)S(1)}, s32[]{:S(2)}) async-start(s8[6291456]{0:T(1024)(128)(4,1)} %bitcast.40), calls=%async_computation.10 | async-start | bytes 8388608
  145.7 4.3 %slice-start.5 = ((s8[6291456]{0:T(1024)(128)(4,1)}), s8[2097152]{0:T(1024)(128)(4,1)S(1)}, s32[]{:S(2)}) async-start(s8[6291456]{0:T(1024)(128)(4,1)} %bitcast.40), calls=%async_computation.11 | async-start | bytes 4194304
  145.7 8.5 %slice-start.2 = ((s8[6291456]{0:T(1024)(128)(4,1)}), s8[4194304]{0:T(1024)(128)(4,1)S(1)}, s32[]{:S(2)}) async-start(s8[6291456]{0:T(1024)(128)(4,1)} %bitcast.38), calls=%async_computation.8 | async-start | bytes 8388608
  150.0 4.2 %slice-start.3 = ((s8[6291456]{0:T(1024)(128)(4,1)}), s8[2097152]{0:T(1024)(128)(4,1)S(1)}, s32[]{:S(2)}) async-start(s8[6291456]{0:T(1024)(128)(4,1)} %bitcast.38), calls=%async_computation.9 | async-start | bytes 4194304
  160.8 184.7 %reduce-scatter.9.cloned.1.call-start = ((), (), s32[]{:S(2)}) async-start(), calls=%async_computation.5 | async-start | bytes 8355840
  178.8 1.1 copy-start.1
Sparse Core Ops, SparseCore 0:
  33.3 137.0 all-gather.1
  173.9 83.8 reduce-scatter.6
  261.2 84.1 reduce-scatter.8
